TPU v7x, 32 devices: a whole 2x2x4 slice. The times are simulated.
32 devices in a mesh: section: 4 (over x, core), expert: 8 (over z, y).
Axes of the slice: x: 2, y: 2, z: 4, core: 2. Of those that a mesh axis runs over, the one named last changes fastest.
Arguments:
- sent_acts: bfloat16 [4, 512, 2048], P('section', 'expert'), may hold values from -6 to 6
- stash: bfloat16 [4, 512, 2048], P('section', 'expert'), may hold values from -6 to 6
- cotangents: bfloat16 [4, 512, 2048], P('section', 'expert'), may hold values from -6 to 6
- norm_gain: bfloat16 [4, 2048], P('section'), may hold values from 0.5 to 1.5
- w_gate: bfloat16 [4, 16, 2048, 768], P('section', 'expert'), may hold values from -0.125 to 0.125
- w_up: bfloat16 [4, 16, 2048, 768], P('section', 'expert'), may hold values from -0.125 to 0.125
- w_down: bfloat16 [4, 16, 768, 2048], P('section', 'expert'), may hold values from -0.21875 to 0.21875
- routes_next: int32 [4, 512, 8], P('section', 'expert'), may hold values from 0 to 15, all different within a row; in each aligned block of 64 rows (0 to 63, 64 to 127, ..., all dimensions but the last counted through in order) at most 48 rows name the same one
- gates_next: bfloat16 [4, 512, 8], P('section', 'expert'), may hold values from 0.049804688 to 0.5
- routes_prev: int32 [4, 512, 8], P('section', 'expert'), may hold values from 0 to 15, all different within a row; in each aligned block of 64 rows (0 to 63, 64 to 127, ..., all dimensions but the last counted through in order) at most 48 rows name the same one
- gates_prev: bfloat16 [4, 512, 8], P('section', 'expert'), may hold values from 0.049804688 to 0.5
Outputs:
- fwd_out: bfloat16 [4, 512, 2048], P('section', 'expert')
- bwd_out: bfloat16 [4, 512, 2048], P('section', 'expert')
- gate_grad: bfloat16 [4, 512, 8], P('section', 'expert')
- grad_w_gate: bfloat16 [4, 16, 2048, 768], P('section', 'expert')
- grad_w_up: bfloat16 [4, 16, 2048, 768], P('section', 'expert')
- grad_w_down: bfloat16 [4, 16, 768, 2048], P('section', 'expert')
Inputs may be any that keep to these rules, and one draw needn't show every extreme that they name: `routes_next`: each row names 8 different experts. At most 48 of the 64 tokens of one device choose one expert, and in some device's tokens some expert is chosen by exactly 48. `routes_prev`: each row names 8 different experts. At most 48 of the 64 tokens of one device choose one expert, and in some device's tokens some expert is chosen by exactly 48.
All inputs are finite; a program needn't handle non-finite values.
Results may differ from a plain program's by a relative error of at most 0.008.
Values may be sent and summed in bfloat16 or wider, within the bound.
A program may use at most 128 MiB of HBM per device.

v0:
```python
import jax
import jax.numpy as jnp
from jax import lax
from jax.sharding import PartitionSpec as P

CAP = 48
EPS = 1e-06


def shifted(array, axis, by):
    count = lax.axis_size(axis)
    return lax.ppermute(array, axis, [(i, (i + by) % count) for i in range(count)])


def apply_rms_norm(rows, norm_scale_weight):
    value_entries = rows.astype(jnp.float32)
    inverse_root_scale = lax.rsqrt(
        jnp.mean(value_entries * value_entries, axis=-1, keepdims=True) + EPS
    )
    unit_rows = value_entries * inverse_root_scale
    normalized_rows = (unit_rows * norm_scale_weight.astype(jnp.float32)).astype(jnp.bfloat16)
    return (normalized_rows, unit_rows, inverse_root_scale)


def routing_tables(routes, experts_all):
    tokens_here, top = routes.shape
    flat = routes.reshape(-1)
    onehot = (flat[:, None] == jnp.arange(experts_all, dtype=jnp.int32)[None, :]).astype(jnp.int32)
    before = jnp.cumsum(onehot, axis=0) - onehot
    slot = jnp.sum(before * onehot, axis=1)
    target = flat * CAP + slot
    pick = (target[:, None] == jnp.arange(experts_all * CAP, dtype=jnp.int32)[None, :]).astype(
        jnp.float32
    )
    spread = jnp.sum(pick.reshape(tokens_here, top, -1), axis=1)
    return (pick, spread)


def pack_rows(spread, rows, experts_all, owners):
    packed = jnp.einsum(
        "tr,td->rd", spread.astype(jnp.bfloat16), rows, preferred_element_type=jnp.float32
    ).astype(jnp.bfloat16)
    return packed.reshape(owners, experts_all // owners, CAP, rows.shape[1])


def slot_values(pick, values):
    return jnp.dot(values.reshape(-1).astype(jnp.float32), pick, precision=lax.Precision.HIGHEST)


def choice_values(pick, values, top):
    return jnp.dot(pick, values.reshape(-1), precision=lax.Precision.HIGHEST).reshape(-1, top)


def expert_inputs(rows, weight_gate, weight_up):
    pre_gate = jnp.einsum("sjcd,jdf->sjcf", rows, weight_gate, preferred_element_type=jnp.float32)
    pre_up = jnp.einsum("sjcd,jdf->sjcf", rows, weight_up, preferred_element_type=jnp.float32)
    return (pre_gate, pre_up)


def expert_outputs(hidden, weight_down):
    return jnp.einsum(
        "sjcf,jfd->sjcd", hidden, weight_down, preferred_element_type=jnp.float32
    ).astype(jnp.bfloat16)


def per_device(
    sent_acts,
    stash,
    cotangents,
    norm_gain,
    w_gate,
    w_up,
    w_down,
    routes_next,
    gates_next,
    routes_prev,
    gates_prev,
):
    owners = lax.axis_size("expert")
    norm_scale_weight = norm_gain[0]
    weight_gate = w_gate[0]
    weight_up = w_up[0]
    weight_down = w_down[0]
    top = routes_next.shape[2]
    width = norm_scale_weight.shape[0]
    experts_all = weight_gate.shape[0] * owners
    tokens_here = routes_next.shape[1]
    arrived = shifted(sent_acts, "section", 1)[0]
    normalized_rows, _, _ = apply_rms_norm(arrived, norm_scale_weight)
    pick, spread = routing_tables(routes_next[0], experts_all)
    send = pack_rows(spread, normalized_rows, experts_all, owners)
    blend = jnp.sum(
        pick.reshape(tokens_here, top, -1) * gates_next[0].astype(jnp.float32)[..., None], axis=1
    ).astype(jnp.bfloat16)
    pre_gate, pre_up = expert_inputs(
        lax.all_to_all(send, "expert", split_axis=0, concat_axis=0, tiled=True),
        weight_gate,
        weight_up,
    )
    hidden = (jax.nn.silu(pre_gate) * pre_up).astype(jnp.bfloat16)
    returned = lax.all_to_all(
        expert_outputs(hidden, weight_down), "expert", split_axis=0, concat_axis=0, tiled=True
    )
    mixed = jnp.dot(
        blend, returned.reshape(experts_all * CAP, width), preferred_element_type=jnp.float32
    )
    fwd_out = (arrived.astype(jnp.float32) + mixed).astype(jnp.bfloat16)
    received_rows = shifted(cotangents, "section", -1)[0]
    previous_normalized_rows, unit_rows, inverse_root_scale = apply_rms_norm(
        stash[0], norm_scale_weight
    )
    pick_prev, spread_prev = routing_tables(routes_prev[0], experts_all)
    rows_send = pack_rows(spread_prev, previous_normalized_rows, experts_all, owners)
    plain_send = pack_rows(spread_prev, received_rows, experts_all, owners)
    gate_slots = (
        slot_values(pick_prev, gates_prev[0])
        .astype(jnp.bfloat16)
        .reshape(owners, experts_all // owners, CAP)
    )
    rows_recv, plain_recv, weight_recv = (
        lax.all_to_all(rows_send, "expert", split_axis=0, concat_axis=0, tiled=True),
        lax.all_to_all(plain_send, "expert", split_axis=0, concat_axis=0, tiled=True),
        lax.all_to_all(gate_slots, "expert", split_axis=0, concat_axis=0, tiled=True),
    )
    grad_recv = (
        weight_recv.astype(jnp.float32)[..., None] * plain_recv.astype(jnp.float32)
    ).astype(jnp.bfloat16)
    pre_gate, pre_up = expert_inputs(rows_recv, weight_gate, weight_up)
    sigma = jax.nn.sigmoid(pre_gate)
    active = pre_gate * sigma
    hidden = (active * pre_up).astype(jnp.bfloat16)
    expert_out = expert_outputs(hidden, weight_down)
    d_hidden = jnp.einsum(
        "sjcd,jfd->sjcf", grad_recv, weight_down, preferred_element_type=jnp.float32
    )
    d_gate = (d_hidden * pre_up * sigma * (1.0 + pre_gate * (1.0 - sigma))).astype(jnp.bfloat16)
    d_up = (d_hidden * active).astype(jnp.bfloat16)
    row_grad = (
        jnp.einsum("sjcf,jdf->sjcd", d_gate, weight_gate, preferred_element_type=jnp.float32)
        + jnp.einsum("sjcf,jdf->sjcd", d_up, weight_up, preferred_element_type=jnp.float32)
    ).astype(jnp.bfloat16)
    grad_gate = jnp.einsum(
        "sjcd,sjcf->jdf", rows_recv, d_gate, preferred_element_type=jnp.float32
    ).astype(jnp.bfloat16)
    grad_up = jnp.einsum(
        "sjcd,sjcf->jdf", rows_recv, d_up, preferred_element_type=jnp.float32
    ).astype(jnp.bfloat16)
    grad_down = jnp.einsum(
        "sjcf,sjcd->jfd", hidden, grad_recv, preferred_element_type=jnp.float32
    ).astype(jnp.bfloat16)
    products = jnp.sum(
        expert_out.astype(jnp.float32) * plain_recv.astype(jnp.float32), axis=-1
    ).astype(jnp.bfloat16)
    grad_back, products_back = (
        lax.all_to_all(row_grad, "expert", split_axis=0, concat_axis=0, tiled=True),
        lax.all_to_all(products, "expert", split_axis=0, concat_axis=0, tiled=True),
    )
    gate_grad = choice_values(pick_prev, products_back.astype(jnp.float32), top).astype(
        jnp.bfloat16
    )
    summed = jnp.dot(
        spread_prev.astype(jnp.bfloat16),
        grad_back.reshape(experts_all * CAP, width),
        preferred_element_type=jnp.float32,
    )
    normalized_gradient = summed * norm_scale_weight.astype(jnp.float32)
    backward_result = received_rows.astype(jnp.float32) + inverse_root_scale * (
        normalized_gradient
        - unit_rows * jnp.mean(normalized_gradient * unit_rows, axis=-1, keepdims=True)
    )
    return (
        fwd_out[None],
        backward_result.astype(jnp.bfloat16)[None],
        gate_grad[None],
        grad_gate[None],
        grad_up[None],
        grad_down[None],
    )


def solution(mesh):
    return jax.shard_map(
        per_device,
        mesh=mesh,
        in_specs=(
            P("section", "expert", None),
            P("section", "expert", None),
            P("section", "expert", None),
            P("section", None),
            P("section", "expert", None, None),
            P("section", "expert", None, None),
            P("section", "expert", None, None),
            P("section", "expert", None),
            P("section", "expert", None),
            P("section", "expert", None),
            P("section", "expert", None),
        ),
        out_specs=(
            P("section", "expert", None),
            P("section", "expert", None),
            P("section", "expert", None),
            P("section", "expert", None, None),
            P("section", "expert", None, None),
            P("section", "expert", None, None),
        ),
        check_vma=False,
    )
```

profile of v0, /device:TPU:0, one launch (start us, length us, event | category | flops | bytes accessed | tf_op | source)
XLA Modules:
  0.0 413.2 jit_solution(9998880206730808746)
XLA Ops:
  0.6 0.8 copy.152
  1.6 1.2 reduce-window.16
  3.0 0.8 copy.156
  4.4 0.7 reshape.169
  5.1 7.3 %all-to-all-start.2 = ((bf16[8,2,48]{2,1,0:T(2,128)(2,1)}), bf16[8,2,48]{2,1,0:T(2,128)(2,1)S(1)}, u32[]{:S(2)}, u32[]{:S(2)}) async-start(bf16[8,2,48]{2,1,0:T(2,128)(2,1)} %reshape.169), calls=%async_computation.2 | async-start | bytes 8192 | tf_op jit(solution)/shard_map/all_to_all | solution.py:123
  12.5 0.7 mul.177
  13.2 1.1 fusion.87
  14.9 3.7 convolution_convert_fusion
  18.9 5.7 %all-to-all-start.4 = ((bf16[8,2,48,2048]{3,2,1,0:T(8,128)(2,1)}), bf16[8,2,48,2048]{3,2,1,0:T(8,128)(2,1)S(1)}, u32[]{:S(2)}, u32[]{:S(2)}) async-start(bf16[8,2,48,2048]{3,2,1,0:T(8,128)(2,1)} %bitcast.29), calls=%async_computation.4 | async-start | bytes 6291456 | tf_op jit(solution)/shard_map/all_to_all | solution.py:121
  24.7 4.2 %collective-permute-done.1 = bf16[1,64,2048]{2,1,0:T(8,128)(2,1)S(1)} collective-permute-done((bf16[1,64,2048]{2,1,0:T(8,128)(2,1)}, bf16[1,64,2048]{2,1,0:T(8,128)(2,1)S(1)}, u32[]{:S(2)}, u32[]{:S(2)}) %collective-permute-start.1) | collective-permute-done | bytes 262176 | tf_op jit(solution)/shard_map/ppermute | solution.py:12
  28.9 2.7 convolution_convert_fusion.1
  31.6 63.2 %all-to-all-done.4 = bf16[8,2,48,2048]{3,2,1,0:T(8,128)(2,1)S(1)} async-done(((bf16[8,2,48,2048]{3,2,1,0:T(8,128)(2,1)}), bf16[8,2,48,2048]{3,2,1,0:T(8,128)(2,1)S(1)}, u32[]{:S(2)}, u32[]{:S(2)}) %all-to-all-start.4) | async-done | bytes 3145760 | tf_op jit(solution)/shard_map/all_to_all | solution.py:121
  94.8 4.6 %all-to-all-start.3 = ((bf16[8,2,48,2048]{3,2,1,0:T(8,128)(2,1)}), bf16[8,2,48,2048]{3,2,1,0:T(8,128)(2,1)}, u32[]{:S(2)}, u32[]{:S(2)}) async-start(bf16[8,2,48,2048]{3,2,1,0:T(8,128)(2,1)} %bitcast.25), calls=%async_computation.3 | async-start | bytes 6291456 | tf_op jit(solution)/shard_map/all_to_all | solution.py:122
  100.9 3.1 reduce-window.14
  104.0 1.6 slice_reduce_fusion.1
  105.6 0.7 reduce-window.15
  106.3 0.9 fusion.108
  107.2 0.7 reduce_sum.86
  107.9 1.4 bitcast_add_fusion.1
  109.3 0.7 bitcast_convert_fusion.4
  110.0 2.4 select_reduce_fusion
  112.6 2.7 convolution_convert_fusion.2
  115.3 54.2 %all-to-all-done.3 = bf16[8,2,48,2048]{3,2,1,0:T(8,128)(2,1)} async-done(((bf16[8,2,48,2048]{3,2,1,0:T(8,128)(2,1)}), bf16[8,2,48,2048]{3,2,1,0:T(8,128)(2,1)}, u32[]{:S(2)}, u32[]{:S(2)}) %all-to-all-start.3) | async-done | bytes 3145760 | tf_op jit(solution)/shard_map/all_to_all | solution.py:122
  169.5 4.6 %all-to-all-start = ((bf16[8,2,48,2048]{3,2,1,0:T(8,128)(2,1)}), bf16[8,2,48,2048]{3,2,1,0:T(8,128)(2,1)}, u32[]{:S(2)}, u32[]{:S(2)}) async-start(bf16[8,2,48,2048]{3,2,1,0:T(8,128)(2,1)} %bitcast.6), calls=%async_computation | async-start | bytes 6291456 | tf_op jit(solution)/shard_map/all_to_all | solution.py:96
  174.2 4.7 %fusion.7 = f32[2,8,48,768]{3,2,1,0:T(8,128)S(1)} fusion(bf16[1,2,2048,768]{3,2,1,0:T(8,128)(2,1)} %param.15, bf16[8,2,48,2048]{3,2,1,0:T(8,128)(2,1)S(1)} %all-to-all-done.4), kind=kOutput, calls=%fused_computation.12 | convolution fusion | flops 2415919104 | bytes 11796480 | tf_op jit(solution)/shard_map/sjcd,jdf->sjcf/dot_general | solution.py:55
  178.9 6.5 %fusion.19 = f32[2,8,48,768]{3,2,1,0:T(8,128)S(1)} fusion(bf16[1,2,768,2048]{3,2,1,0:T(8,128)(2,1)} %param.17, f32[8,2,48]{2,0,1:T(8,128)S(1)} %copy_convert_fusion, bf16[8,2,48,2048]{3,2,1,0:T(8,128)(2,1)} %all-to-all-done.3), kind=kOutput, calls=%fused_computation.24 | convolution fusion | flops 2420637696 | bytes 11799552 | tf_op jit(solution)/shard_map/sjcd,jfd->sjcf/dot_general | solution.py:133
  185.5 7.4 %fusion.50 = (bf16[8,2,48,768]{3,2,0,1:T(8,128)(2,1)S(1)}, bf16[8,2,48,768]{3,2,0,1:T(8,128)(2,1)S(1)}, bf16[8,2,48,768]{3,2,0,1:T(8,128)(2,1)}) fusion(f32[2,8,48,768]{3,2,1,0:T(8,128)S(1)} %fusion.7, f32[2,8,48,768]{3,2,1,0:T(8,128)S(1)} %fusion.19, bf16[1,2,2048,768]{3,2,1,0:T(8,128)(2,1)} %param.16, bf16[8,2,48,2048]{3,2,1,0:T(8,128)(2,1)S(1)} %all-to-all-done.4), kind=kOutput, calls=%fused_computation.52 | convolution fusion | flops 2424766464 | bytes 17694720 | tf_op jit(solution)/shard_map/sjcd,jdf->sjcf/dot_general | solution.py:56
  192.9 5.3 %fusion.1 = bf16[8,2,48]{2,0,1:T(8,128)(2,1)S(1)} fusion(bf16[8,2,48,2048]{3,2,1,0:T(8,128)(2,1)} %all-to-all-done.3, bf16[8,2,48,768]{3,2,0,1:T(8,128)(2,1)S(1)} %get-tuple-element.8, bf16[1,2,768,2048]{3,2,1,0:T(8,128)(2,1)S(1)} %bitcast.239), kind=kOutput, calls=%fused_computation.6 | convolution fusion | flops 2423782656 | bytes 10618368 | tf_op jit(solution)/shard_map/sjcf,jfd->sjcd/dot_general | solution.py:61
  198.8 4.5 %fusion.5 = f32[2,8,48,2048]{3,2,1,0:T(8,128)} fusion(bf16[8,2,48,768]{3,2,0,1:T(8,128)(2,1)S(1)} %get-tuple-element.9, bf16[1,2,2048,768]{3,2,1,0:T(8,128)(2,1)S(1)} %bitcast.237), kind=kOutput, calls=%fused_computation.10 | convolution fusion | flops 2415919104 | bytes 13762560 | tf_op jit(solution)/shard_map/sjcf,jdf->sjcd/dot_general | solution.py:139
  203.3 41.0 %all-to-all-done = bf16[8,2,48,2048]{3,2,1,0:T(8,128)(2,1)} async-done(((bf16[8,2,48,2048]{3,2,1,0:T(8,128)(2,1)}), bf16[8,2,48,2048]{3,2,1,0:T(8,128)(2,1)}, u32[]{:S(2)}, u32[]{:S(2)}) %all-to-all-start) | async-done | bytes 3145760 | tf_op jit(solution)/shard_map/all_to_all | solution.py:96
  244.3 3.5 all-to-all-start.6
  247.8 8.2 %fusion.34 = bf16[8,2,48,2048]{3,2,0,1:T(8,128)(2,1)S(1)} fusion(f32[2,8,48,2048]{3,2,1,0:T(8,128)} %fusion.5, bf16[8,2,48,768]{3,2,0,1:T(8,128)(2,1)S(1)} %copy-done.12, bf16[1,2,2048,768]{3,2,1,0:T(8,128)(2,1)} %param.16), kind=kOutput, calls=%fused_computation.35 | convolution fusion | flops 2419064832 | bytes 16908288 | tf_op jit(solution)/shard_map/sjcf,jdf->sjcd/dot_general | solution.py:140
  256.0 1.9 copy.161
  257.9 6.0 %all-to-all-start.5 = ((bf16[8,2,48,2048]{3,2,1,0:T(8,128)(2,1)}), bf16[8,2,48,2048]{3,2,1,0:T(8,128)(2,1)S(1)}, u32[]{:S(2)}, u32[]{:S(2)}) async-start(bf16[8,2,48,2048]{3,2,1,0:T(8,128)(2,1)} %copy.161), calls=%async_computation.5 | async-start | bytes 6291456 | tf_op jit(solution)/shard_map/all_to_all | solution.py:155
  263.8 7.7 %fusion.9 = f32[2,8,48,768]{3,2,1,0:T(8,128)} fusion(bf16[1,2,2048,768]{3,2,1,0:T(8,128)(2,1)} %param.15, bf16[8,2,48,2048]{3,2,1,0:T(8,128)(2,1)} %all-to-all-done), kind=kOutput, calls=%fused_computation.14 | convolution fusion | flops 2415919104 | bytes 11796480 | tf_op jit(solution)/shard_map/sjcd,jdf->sjcf/dot_general | solution.py:55
  271.6 13.0 %fusion.31 = bf16[8,2,48,2048]{3,2,0,1:T(8,128)(2,1)} fusion(bf16[1,2,768,2048]{3,2,1,0:T(8,128)(2,1)} %param.17, f32[2,8,48,768]{3,2,1,0:T(8,128)} %fusion.9, bf16[1,2,2048,768]{3,2,1,0:T(8,128)(2,1)} %param.16, bf16[8,2,48,2048]{3,2,1,0:T(8,128)(2,1)} %all-to-all-done), kind=kOutput, calls=%fused_computation.34 | convolution fusion | flops 4836950016 | bytes 21233664 | tf_op jit(solution)/shard_map/sjcf,jfd->sjcd/dot_general | solution.py:61
  284.6 4.0 copy.151
  288.6 45.6 %all-to-all-done.5 = bf16[8,2,48,2048]{3,2,1,0:T(8,128)(2,1)S(1)} async-done(((bf16[8,2,48,2048]{3,2,1,0:T(8,128)(2,1)}), bf16[8,2,48,2048]{3,2,1,0:T(8,128)(2,1)S(1)}, u32[]{:S(2)}, u32[]{:S(2)}) %all-to-all-start.5) | async-done | bytes 3145760 | tf_op jit(solution)/shard_map/all_to_all | solution.py:155
  334.2 4.7 %all-to-all-start.1 = ((bf16[8,2,48,2048]{3,2,1,0:T(8,128)(2,1)}), bf16[8,2,48,2048]{3,2,1,0:T(8,128)(2,1)}, u32[]{:S(2)}, u32[]{:S(2)}) async-start(bf16[8,2,48,2048]{3,2,1,0:T(8,128)(2,1)} %copy.151), calls=%async_computation.1 | async-start | bytes 6291456 | tf_op jit(solution)/shard_map/all_to_all | solution.py:101
  338.9 8.6 %fusion.4 = bf16[1,2,768,2048]{3,2,1,0:T(8,128)(2,1)} fusion(bf16[8,2,48,768]{3,2,0,1:T(8,128)(2,1)} %copy-done.16, f32[8,2,48]{2,0,1:T(8,128)S(1)} %copy_convert_fusion, bf16[8,2,48,2048]{3,2,1,0:T(8,128)(2,1)} %all-to-all-done.3), kind=kOutput, calls=%fused_computation.9 | convolution fusion | flops 2423783424 | bytes 10619904 | tf_op jit(solution)/shard_map/sjcf,sjcd->jfd/dot_general | solution.py:148
  347.6 5.4 %fusion.2 = bf16[1,2,2048,768]{3,2,1,0:T(8,128)(2,1)} fusion(bf16[8,2,48,2048]{3,2,1,0:T(8,128)(2,1)S(1)} %copy-done.2, bf16[8,2,48,768]{3,2,0,1:T(8,128)(2,1)S(1)} %copy-done.15), kind=kOutput, calls=%fused_computation.7 | convolution fusion | flops 2419064832 | bytes 10616832 | tf_op jit(solution)/shard_map/sjcd,sjcf->jdf/dot_general | solution.py:142
  353.0 5.4 %fusion.3 = bf16[1,2,2048,768]{3,2,1,0:T(8,128)(2,1)} fusion(bf16[8,2,48,2048]{3,2,1,0:T(8,128)(2,1)S(1)} %copy-done.2, bf16[8,2,48,768]{3,2,0,1:T(8,128)(2,1)S(1)} %copy-done.13), kind=kOutput, calls=%fused_computation.8 | convolution fusion | flops 2419064832 | bytes 10616832 | tf_op jit(solution)/shard_map/sjcd,sjcf->jdf/dot_general | solution.py:145
  359.1 3.2 fusion.70
  362.3 0.8 copy.168
  363.7 1.6 fusion.82
  365.3 43.6 %all-to-all-done.1 = bf16[8,2,48,2048]{3,2,1,0:T(8,128)(2,1)} async-done(((bf16[8,2,48,2048]{3,2,1,0:T(8,128)(2,1)}), bf16[8,2,48,2048]{3,2,1,0:T(8,128)(2,1)}, u32[]{:S(2)}, u32[]{:S(2)}) %all-to-all-start.1) | async-done | bytes 3145760 | tf_op jit(solution)/shard_map/all_to_all | solution.py:101
  409.0 3.3 fusion.57
  412.3 0.9 fusion.92
  (76 shorter events, 5.8 us)
Async XLA Ops:
  5.1 13.7 %all-to-all-start.2 = ((bf16[8,2,48]{2,1,0:T(2,128)(2,1)}), bf16[8,2,48]{2,1,0:T(2,128)(2,1)S(1)}, u32[]{:S(2)}, u32[]{:S(2)}) async-start(bf16[8,2,48]{2,1,0:T(2,128)(2,1)} %reshape.169), calls=%async_computation.2 | async-start | bytes 8192 | tf_op jit(solution)/shard_map/all_to_all | solution.py:123
  14.4 4.5 %copy-start.9 = (f32[64]{0:T(128)}, f32[64]{0:T(128)S(1)}, u32[]{:S(2)}) copy-start(f32[64]{0:T(128)S(1)} %add_rsqrt_fusion) | copy-start | bytes 772
  14.4 4.5 %copy-start.7 = (s32[64,8]{1,0:T(8,128)}, s32[64,8]{1,0:T(8,128)S(1)}, u32[]{:S(2)}) copy-start(s32[64,8]{1,0:T(8,128)S(1)} %bitcast_add_fusion) | copy-start | bytes 6148
  18.9 75.9 %all-to-all-start.4 = ((bf16[8,2,48,2048]{3,2,1,0:T(8,128)(2,1)}), bf16[8,2,48,2048]{3,2,1,0:T(8,128)(2,1)S(1)}, u32[]{:S(2)}, u32[]{:S(2)}) async-start(bf16[8,2,48,2048]{3,2,1,0:T(8,128)(2,1)} %bitcast.29), calls=%async_computation.4 | async-start | bytes 6291456 | tf_op jit(solution)/shard_map/all_to_all | solution.py:121
  24.6 4.3 %collective-permute-start.1 = (bf16[1,64,2048]{2,1,0:T(8,128)(2,1)}, bf16[1,64,2048]{2,1,0:T(8,128)(2,1)S(1)}, u32[]{:S(2)}, u32[]{:S(2)}) collective-permute-start(bf16[1,64,2048]{2,1,0:T(8,128)(2,1)} %param.13), channel_id=1, source_target_pairs={{0,24},{8,0},{16,8},{24,16},{1,25},{9,1},{17,9},{25,17},{2,26},{10... | collective-permute-start | bytes 786440 | tf_op jit(solution)/shard_map/ppermute | solution.py:12
  28.9 65.9 %copy-start.5 = (bf16[1,64,2048]{2,1,0:T(8,128)(2,1)}, bf16[1,64,2048]{2,1,0:T(8,128)(2,1)S(1)}, u32[]{:S(2)}) copy-start(bf16[1,64,2048]{2,1,0:T(8,128)(2,1)S(1)} %collective-permute-done.1) | copy-start | bytes 786436
  94.8 90.7 %copy-start.1 = (bf16[8,2,48,2048]{3,2,1,0:T(8,128)(2,1)}, bf16[8,2,48,2048]{3,2,1,0:T(8,128)(2,1)S(1)}, u32[]{:S(2)}) copy-start(bf16[8,2,48,2048]{3,2,1,0:T(8,128)(2,1)S(1)} %all-to-all-done.4) | copy-start | bytes 9437188
  94.8 4.7 %copy-start.11 = (s32[1,64,8]{1,2,0:T(8,128)S(1)}, s32[1,64,8]{1,2,0:T(8,128)}, u32[]{:S(2)}) copy-start(s32[1,64,8]{1,2,0:T(8,128)} %param.18) | copy-start | bytes 6148
  94.8 74.8 %all-to-all-start.3 = ((bf16[8,2,48,2048]{3,2,1,0:T(8,128)(2,1)}), bf16[8,2,48,2048]{3,2,1,0:T(8,128)(2,1)}, u32[]{:S(2)}, u32[]{:S(2)}) async-start(bf16[8,2,48,2048]{3,2,1,0:T(8,128)(2,1)} %bitcast.25), calls=%async_computation.3 | async-start | bytes 6291456 | tf_op jit(solution)/shard_map/all_to_all | solution.py:122
  99.3 13.1 %collective-permute-start = (bf16[1,64,2048]{2,1,0:T(8,128)(2,1)}, bf16[1,64,2048]{2,1,0:T(8,128)(2,1)S(1)}, u32[]{:S(2)}, u32[]{:S(2)}) collective-permute-start(bf16[1,64,2048]{2,1,0:T(8,128)(2,1)} %param.11), channel_id=1, source_target_pairs={{0,8},{8,16},{16,24},{24,0},{1,9},{9,17},{17,25},{25,1},{2,10},{10... | collective-permute-start | bytes 786440 | tf_op jit(solution)/shard_map/ppermute | solution.py:12
  112.5 57.1 %copy-start.3 = (bf16[1,64,2048]{2,1,0:T(8,128)(2,1)}, bf16[1,64,2048]{2,1,0:T(8,128)(2,1)S(1)}, u32[]{:S(2)}) copy-start(bf16[1,64,2048]{2,1,0:T(8,128)(2,1)S(1)} %collective-permute-done) | copy-start | bytes 786436
  169.5 74.7 %all-to-all-start = ((bf16[8,2,48,2048]{3,2,1,0:T(8,128)(2,1)}), bf16[8,2,48,2048]{3,2,1,0:T(8,128)(2,1)}, u32[]{:S(2)}, u32[]{:S(2)}) async-start(bf16[8,2,48,2048]{3,2,1,0:T(8,128)(2,1)} %bitcast.6), calls=%async_computation | async-start | bytes 6291456 | tf_op jit(solution)/shard_map/all_to_all | solution.py:96
  178.9 14.0 %slice-start.2 = ((s8[6291456]{0:T(1024)(128)(4,1)}), s8[4194304]{0:T(1024)(128)(4,1)S(1)}, s32[]{:S(2)}) async-start(s8[6291456]{0:T(1024)(128)(4,1)} %bitcast.238), calls=%async_computation.9 | async-start | bytes 8388608
  178.9 19.9 %slice-start = ((s8[6291456]{0:T(1024)(128)(4,1)}), s8[2097152]{0:T(1024)(128)(4,1)S(1)}, s32[]{:S(2)}) async-start(s8[6291456]{0:T(1024)(128)(4,1)} %bitcast.236), calls=%async_computation.7 | async-start | bytes 4194304
  185.4 7.4 %slice-start.3 = ((s8[6291456]{0:T(1024)(128)(4,1)}), s8[2097152]{0:T(1024)(128)(4,1)S(1)}, s32[]{:S(2)}) async-start(s8[6291456]{0:T(1024)(128)(4,1)} %bitcast.238), calls=%async_computation.10 | async-start | bytes 4194304
  185.5 13.3 %slice-start.1 = ((s8[6291456]{0:T(1024)(128)(4,1)}), s8[4194304]{0:T(1024)(128)(4,1)S(1)}, s32[]{:S(2)}) async-start(s8[6291456]{0:T(1024)(128)(4,1)} %bitcast.236), calls=%async_computation.8 | async-start | bytes 8388608
  192.8 5.3 %copy-start.16 = (bf16[8,2,48,768]{3,2,0,1:T(8,128)(2,1)}, bf16[8,2,48,768]{3,2,0,1:T(8,128)(2,1)S(1)}, u32[]{:S(2)}) copy-start(bf16[8,2,48,768]{3,2,0,1:T(8,128)(2,1)S(1)} %get-tuple-element.8) | copy-start | bytes 3538948
  192.8 5.9 %copy-start.14 = (bf16[8,2,48,768]{3,2,0,1:T(8,128)(2,1)}, bf16[8,2,48,768]{3,2,0,1:T(8,128)(2,1)S(1)}, u32[]{:S(2)}) copy-start(bf16[8,2,48,768]{3,2,0,1:T(8,128)(2,1)S(1)} %get-tuple-element.9) | copy-start | bytes 3538948
  198.8 49.0 %copy-start.12 = (bf16[8,2,48,768]{3,2,0,1:T(8,128)(2,1)S(1)}, bf16[8,2,48,768]{3,2,0,1:T(8,128)(2,1)}, u32[]{:S(2)}) copy-start(bf16[8,2,48,768]{3,2,0,1:T(8,128)(2,1)} %get-tuple-element.10) | copy-start | bytes 3538948
  244.3 13.6 %all-to-all-start.6 = ((bf16[8,2,48]{2,1,0:T(2,128)(2,1)}), bf16[8,2,48]{2,1,0:T(2,128)(2,1)S(1)}, u32[]{:S(2)}, u32[]{:S(2)}) async-start(bf16[8,2,48]{2,1,0:T(2,128)(2,1)} %copy.162), calls=%async_computation.6 | async-start | bytes 8192 | tf_op jit(solution)/shard_map/all_to_all | solution.py:156
  257.9 76.3 %all-to-all-start.5 = ((bf16[8,2,48,2048]{3,2,1,0:T(8,128)(2,1)}), bf16[8,2,48,2048]{3,2,1,0:T(8,128)(2,1)S(1)}, u32[]{:S(2)}, u32[]{:S(2)}) async-start(bf16[8,2,48,2048]{3,2,1,0:T(8,128)(2,1)} %copy.161), calls=%async_computation.5 | async-start | bytes 6291456 | tf_op jit(solution)/shard_map/all_to_all | solution.py:155
  334.2 74.8 %all-to-all-start.1 = ((bf16[8,2,48,2048]{3,2,1,0:T(8,128)(2,1)}), bf16[8,2,48,2048]{3,2,1,0:T(8,128)(2,1)}, u32[]{:S(2)}, u32[]{:S(2)}) async-start(bf16[8,2,48,2048]{3,2,1,0:T(8,128)(2,1)} %copy.151), calls=%async_computation.1 | async-start | bytes 6291456 | tf_op jit(solution)/shard_map/all_to_all | solution.py:101
  338.9 8.7 %copy-start.2 = (bf16[8,2,48,2048]{3,2,1,0:T(8,128)(2,1)S(1)}, bf16[8,2,48,2048]{3,2,1,0:T(8,128)(2,1)}, u32[]{:S(2)}) copy-start(bf16[8,2,48,2048]{3,2,1,0:T(8,128)(2,1)} %copy-done.1) | copy-start | bytes 9437188
  338.9 8.7 %copy-start.15 = (bf16[8,2,48,768]{3,2,0,1:T(8,128)(2,1)S(1)}, bf16[8,2,48,768]{3,2,0,1:T(8,128)(2,1)}, u32[]{:S(2)}) copy-start(bf16[8,2,48,768]{3,2,0,1:T(8,128)(2,1)} %copy-done.14) | copy-start | bytes 3538948
  347.6 5.4 %copy-start.13 = (bf16[8,2,48,768]{3,2,0,1:T(8,128)(2,1)S(1)}, bf16[8,2,48,768]{3,2,0,1:T(8,128)(2,1)}, u32[]{:S(2)}) copy-start(bf16[8,2,48,768]{3,2,0,1:T(8,128)(2,1)} %get-tuple-element.10) | copy-start | bytes 3538948
  353.0 6.1 %copy-start.8 = (s32[64,8]{1,0:T(8,128)S(1)}, s32[64,8]{1,0:T(8,128)}, u32[]{:S(2)}) copy-start(s32[64,8]{1,0:T(8,128)} %copy-done.7) | copy-start | bytes 6148
  353.0 10.7 %copy-start = (bf16[1,64,2048]{2,1,0:T(8,128)(2,1)S(1)}, bf16[1,64,2048]{2,1,0:T(8,128)(2,1)}, u32[]{:S(2)}) copy-start(bf16[1,64,2048]{2,1,0:T(8,128)(2,1)} %param.12) | copy-start | bytes 786436
  353.0 10.7 %copy-start.10 = (f32[64]{0:T(128)S(1)}, f32[64]{0:T(128)}, u32[]{:S(2)}) copy-start(f32[64]{0:T(128)} %copy-done.9) | copy-start | bytes 772
  365.3 47.0 %copy-start.4 = (f32[64,2048]{1,0:T(8,128)S(1)}, f32[64,2048]{1,0:T(8,128)}, u32[]{:S(2)}) copy-start(f32[64,2048]{1,0:T(8,128)} %get-tuple-element.12) | copy-start | bytes 1572868
  365.3 47.0 %copy-start.6 = (bf16[1,64,2048]{2,1,0:T(8,128)(2,1)S(1)}, bf16[1,64,2048]{2,1,0:T(8,128)(2,1)}, u32[]{:S(2)}) copy-start(bf16[1,64,2048]{2,1,0:T(8,128)(2,1)} %copy-done.5) | copy-start | bytes 786436
where the time goes:
time: 415 us; the launch traced here: 413 us
  waiting for transfers between devices  252 us (61%)
  matrix products  94.3 us (23%)
  starting transfers between devices  36.6 us (9%)
  local copies, waits for them, and re-layouts  14.7 us (4%)
  other arithmetic  14.6 us (4%)
    all_to_all x1, waiting for transfers between devices, per_device(): lax.all_to_all(rows_send, 'expert', split_axis=0, concat_axis=0, tiled=True)  63.2 us
    all_to_all x1, waiting for transfers between devices, per_device(): lax.all_to_all(plain_send, 'expert', split_axis=0, concat_axis=0, tiled=T...  54.2 us
    all_to_all x1, waiting for transfers between devices, per_device(): lax.all_to_all(row_grad, 'expert', split_axis=0, concat_axis=0, tiled=True)  45.6 us
    all_to_all x1, waiting for transfers between devices, per_device(): lax.all_to_all(expert_outputs(hidden, weight_down), 'expert', split_axis=...  43.6 us
    all_to_all x1, waiting for transfers between devices, per_device(): lax.all_to_all(send, 'expert', split_axis=0, concat_axis=0, tiled=True)  41 us
    dot_general x2, matrix products, expert_outputs(): jnp.einsum('sjcf,jfd->sjcd', hidden, weight_down, preferred_element_type=...  18.3 us
    dot_general x2, matrix products, expert_inputs(): jnp.einsum('sjcd,jdf->sjcf', rows, weight_gate, preferred_element_type=jn...  12.4 us
    dot_general x3, matrix products, pack_rows(): jnp.einsum('tr,td->rd', spread.astype(jnp.bfloat16), rows, preferred_elem...  9.02 us
  transfers between devices with their start and end apart: 9, of which 7 were waited for; matrix products, arithmetic and copies ran while one was open for 28% of the time, Pallas kernels for 0%

commit v1 on v0

--- a/solution.py
+++ b/solution.py
@@ -5,6 +5,22 @@
 
 CAP = 48
 EPS = 1e-06
+
+
+def swapped_with_each(array, axis, split, join):
+    ways, here = (lax.axis_size(axis), lax.axis_index(axis))
+    width = array.shape[split] // ways
+    dims = list(array.shape)
+    dims[split] = width
+    height = dims[join]
+    dims[join] = height * ways
+    full = jnp.zeros(dims, array.dtype)
+    for mask in range(ways):
+        part = lax.dynamic_slice_in_dim(array, (here ^ mask) * width, width, axis=split)
+        if mask:
+            part = lax.ppermute(part, axis, [(d, d ^ mask) for d in range(ways)])
+        full = lax.dynamic_update_slice_in_dim(full, part, (here ^ mask) * height, axis=join)
+    return full
 
 
 def shifted(array, axis, by):
@@ -93,9 +109,7 @@
         pick.reshape(tokens_here, top, -1) * gates_next[0].astype(jnp.float32)[..., None], axis=1
     ).astype(jnp.bfloat16)
     pre_gate, pre_up = expert_inputs(
-        lax.all_to_all(send, "expert", split_axis=0, concat_axis=0, tiled=True),
-        weight_gate,
-        weight_up,
+        swapped_with_each(send, "expert", 0, 0), weight_gate, weight_up
     )
     hidden = (jax.nn.silu(pre_gate) * pre_up).astype(jnp.bfloat16)
     returned = lax.all_to_all(

time: 415 us -> 440 us (1.060)
  starting transfers between devices: 36.6 us -> 70.7 us
  matrix products: 94.3 us -> 87 us
    ppermute x0 -> x7, waiting for transfers between devices: none -> 88.5 us  [swapped_with_each(): part = lax.ppermute(part, axis, [(d, d ^ mask) for d in range(ways)])]
    all_to_all x1, waiting for transfers between devices: 54.2 us -> 0.01 us  [per_device(): lax.all_to_all(plain_send, 'expert', split_axis=0, concat_axis=0, tiled=T...]
    all_to_all x1 -> x0, waiting for transfers between devices: 41 us -> none  [per_device(): lax.all_to_all(send, 'expert', split_axis=0, concat_axis=0, tiled=True)]
    ppermute x0 -> x7, starting transfers between devices: none -> 23.4 us  [swapped_with_each(): part = lax.ppermute(part, axis, [(d, d ^ mask) for d in range(ways)])]
    all_to_all x1, starting transfers between devices: 3.54 us -> 18.4 us  [per_device(): lax.all_to_all(products, 'expert', split_axis=0, concat_axis=0, tiled=True)]
    all_to_all x1, waiting for transfers between devices: 43.6 us -> 55.9 us  [per_device(): lax.all_to_all(expert_outputs(hidden, weight_down), 'expert', split_axis=...]
    all_to_all x1 -> x0, starting transfers between devices: 4.62 us -> none  [per_device(): lax.all_to_all(send, 'expert', split_axis=0, concat_axis=0, tiled=True)]
  transfers between devices with their start and end apart: 9 -> 15, of which waited for: 7 -> 10; matrix products, arithmetic and copies ran while one was open for 28% -> 20% of each run, Pallas kernels for 0% -> 0%
where the time goes in v1:
time: 440 us; the launch traced here: 439 us
  waiting for transfers between devices  249 us (57%)
  matrix products  87 us (20%)
  starting transfers between devices  70.7 us (16%)
  other arithmetic  15.5 us (4%)
  local copies, waits for them, and re-layouts  15.4 us (4%)
    ppermute x7, waiting for transfers between devices, swapped_with_each(): part = lax.ppermute(part, axis, [(d, d ^ mask) for d in range(ways)])  88.5 us
    all_to_all x1, waiting for transfers between devices, per_device(): lax.all_to_all(rows_send, 'expert', split_axis=0, concat_axis=0, tiled=True)  60.3 us
    all_to_all x1, waiting for transfers between devices, per_device(): lax.all_to_all(expert_outputs(hidden, weight_down), 'expert', split_axis=...  55.9 us
    all_to_all x1, waiting for transfers between devices, per_device(): lax.all_to_all(row_grad, 'expert', split_axis=0, concat_axis=0, tiled=True)  42.9 us
    ppermute x7, starting transfers between devices, swapped_with_each(): part = lax.ppermute(part, axis, [(d, d ^ mask) for d in range(ways)])  23.4 us
    all_to_all x1, starting transfers between devices, per_device(): lax.all_to_all(products, 'expert', split_axis=0, concat_axis=0, tiled=True)  18.4 us
    dot_general x2, matrix products, expert_outputs(): jnp.einsum('sjcf,jfd->sjcd', hidden, weight_down, preferred_element_type=...  16.1 us
  transfers between devices with their start and end apart: 15, of which 10 were waited for; matrix products, arithmetic and copies ran while one was open for 20% of the time, Pallas kernels for 0%

profile of v1, /device:TPU:0, one launch (start us, length us, event | category | flops | bytes accessed | tf_op | source)
XLA Modules:
  0.0 438.5 jit_solution(16353623859850918830)
XLA Ops:
  1.6 1.2 reduce-window.16
  5.1 7.3 %all-to-all-start.1 = ((bf16[8,2,48]{2,1,0:T(2,128)(2,1)}), bf16[8,2,48]{2,1,0:T(2,128)(2,1)S(1)}, u32[]{:S(2)}, u32[]{:S(2)}) async-start(bf16[8,2,48]{2,1,0:T(2,128)(2,1)} %reshape.169), calls=%async_computation.1 | async-start | bytes 8192 | tf_op jit(solution)/shard_map/all_to_all | solution.py:137
  13.8 1.1 fusion.81
  14.9 3.7 convolution_convert_fusion
  18.9 5.8 %all-to-all-start.3 = ((bf16[8,2,48,2048]{3,2,1,0:T(8,128)(2,1)}), bf16[8,2,48,2048]{3,2,1,0:T(8,128)(2,1)S(1)}, u32[]{:S(2)}, u32[]{:S(2)}) async-start(bf16[8,2,48,2048]{3,2,1,0:T(8,128)(2,1)} %bitcast.29), calls=%async_computation.3 | async-start | bytes 6291456 | tf_op jit(solution)/shard_map/all_to_all | solution.py:135
  26.6 3.1 reduce-window.14
  29.7 1.1 collective-permute-done.8
  30.8 3.6 convolution_convert_fusion.1
  34.4 60.3 %all-to-all-done.3 = bf16[8,2,48,2048]{3,2,1,0:T(8,128)(2,1)S(1)} async-done(((bf16[8,2,48,2048]{3,2,1,0:T(8,128)(2,1)}), bf16[8,2,48,2048]{3,2,1,0:T(8,128)(2,1)S(1)}, u32[]{:S(2)}, u32[]{:S(2)}) %all-to-all-start.3) | async-done | bytes 3145760 | tf_op jit(solution)/shard_map/all_to_all | solution.py:135
  94.8 4.6 %all-to-all-start.2 = ((bf16[8,2,48,2048]{3,2,1,0:T(8,128)(2,1)}), bf16[8,2,48,2048]{3,2,1,0:T(8,128)(2,1)}, u32[]{:S(2)}, u32[]{:S(2)}) async-start(bf16[8,2,48,2048]{3,2,1,0:T(8,128)(2,1)} %bitcast.25), calls=%async_computation.2 | async-start | bytes 6291456 | tf_op jit(solution)/shard_map/all_to_all | solution.py:136
  99.4 1.6 slice_reduce_fusion.1
  103.2 1.4 bitcast_add_fusion.1
  105.4 2.4 select_reduce_fusion
  108.0 1.1 convolution_convert_fusion.2
  109.3 1.8 collective-permute-start.1
  111.1 1.5 collective-permute-start.2
  112.9 2.6 collective-permute-start.4
  115.5 1.4 collective-permute-start.5
  117.4 16.5 %collective-permute-done.1 = bf16[1,2,48,2048]{3,2,0,1:T(8,128)(2,1)S(1)} collective-permute-done((bf16[1,2,48,2048]{3,2,0,1:T(8,128)(2,1)S(1)}, bf16[1,2,48,2048]{3,2,0,1:T(8,128)(2,1)S(1)}, u32[]{:S(2)}, u32[]{:S(2)}) %collective-permute-start.1) | collective-permute-done | bytes 393248 | tf_op jit(solution)/shard_map/ppermute | solution.py:21
  133.9 12.0 %collective-permute-start.6 = (bf16[1,2,48,2048]{3,2,0,1:T(8,128)(2,1)S(1)}, bf16[1,2,48,2048]{3,2,0,1:T(8,128)(2,1)S(1)}, u32[]{:S(2)}, u32[]{:S(2)}) collective-permute-start(bf16[1,2,48,2048]{3,2,0,1:T(8,128)(2,1)S(1)} %get-tuple-element.12), channel_id=1, source_target_pairs={{0,6},{1,7},{2,4},{3,5},{4,2},{5,3},{6,0},{7,1},{8,14},{9,15},{10,... | collective-permute-start | bytes 1179656 | tf_op jit(solution)/shard_map/ppermute | solution.py:21
  145.9 14.5 %collective-permute-done.2 = bf16[1,2,48,2048]{3,2,0,1:T(8,128)(2,1)S(1)} collective-permute-done((bf16[1,2,48,2048]{3,2,0,1:T(8,128)(2,1)S(1)}, bf16[1,2,48,2048]{3,2,0,1:T(8,128)(2,1)S(1)}, u32[]{:S(2)}, u32[]{:S(2)}) %collective-permute-start.2) | collective-permute-done | bytes 393248 | tf_op jit(solution)/shard_map/ppermute | solution.py:21
  160.4 3.8 collective-permute-start.7
  164.2 4.6 %collective-permute-done.3 = bf16[1,2,48,2048]{3,2,0,1:T(8,128)(2,1)S(1)} collective-permute-done((bf16[1,2,48,2048]{3,2,0,1:T(8,128)(2,1)S(1)}, bf16[1,2,48,2048]{3,2,0,1:T(8,128)(2,1)S(1)}, u32[]{:S(2)}, u32[]{:S(2)}) %collective-permute-start.3) | collective-permute-done | bytes 393248 | tf_op jit(solution)/shard_map/ppermute | solution.py:21
  168.9 44.5 %collective-permute-done.4 = bf16[1,2,48,2048]{3,2,0,1:T(8,128)(2,1)S(1)} collective-permute-done((bf16[1,2,48,2048]{3,2,0,1:T(8,128)(2,1)S(1)}, bf16[1,2,48,2048]{3,2,0,1:T(8,128)(2,1)S(1)}, u32[]{:S(2)}, u32[]{:S(2)}) %collective-permute-start.4) | collective-permute-done | bytes 393248 | tf_op jit(solution)/shard_map/ppermute | solution.py:21
  213.5 8.4 %collective-permute-done.5 = bf16[1,2,48,2048]{3,2,0,1:T(8,128)(2,1)S(1)} collective-permute-done((bf16[1,2,48,2048]{3,2,0,1:T(8,128)(2,1)S(1)}, bf16[1,2,48,2048]{3,2,0,1:T(8,128)(2,1)S(1)}, u32[]{:S(2)}, u32[]{:S(2)}) %collective-permute-start.5) | collective-permute-done | bytes 393248 | tf_op jit(solution)/shard_map/ppermute | solution.py:21
  222.0 1.7 copy-done.3
  223.6 4.0 fusion.9
  227.7 4.0 fusion.7
  231.7 6.5 %fusion.19 = f32[2,8,48,768]{3,2,1,0:T(8,128)S(1)} fusion(bf16[1,2,768,2048]{3,2,1,0:T(8,128)(2,1)} %param.17, f32[8,2,48]{2,0,1:T(8,128)S(1)} %copy_convert_fusion, bf16[8,2,48,2048]{3,2,1,0:T(8,128)(2,1)} %all-to-all-done.2), kind=kOutput, calls=%fused_computation.24 | convolution fusion | flops 2420637696 | bytes 11799552 | tf_op jit(solution)/shard_map/sjcd,jfd->sjcf/dot_general | solution.py:147
  238.2 7.4 %fusion.48 = (bf16[8,2,48,768]{3,2,0,1:T(8,128)(2,1)S(1)}, bf16[8,2,48,768]{3,2,0,1:T(8,128)(2,1)}, bf16[8,2,48,768]{3,2,0,1:T(8,128)(2,1)}) fusion(f32[2,8,48,768]{3,2,1,0:T(8,128)S(1)} %copy-done.13, f32[2,8,48,768]{3,2,1,0:T(8,128)S(1)} %fusion.19, bf16[1,2,2048,768]{3,2,1,0:T(8,128)(2,1)} %param.16, bf16[8,2,48,2048]{3,2,1,0:T(8,128)(2,1)S(1)} %all-to-all-done.3), kind=kOutput, calls=%fused_computation.50 | convolution fusion | flops 2424766464 | bytes 17694720 | tf_op jit(solution)/shard_map/sjcd,jdf->sjcf/dot_general | solution.py:72
  245.7 4.8 %fusion.1 = bf16[8,2,48]{2,0,1:T(8,128)(2,1)S(1)} fusion(bf16[8,2,48,2048]{3,2,1,0:T(8,128)(2,1)} %all-to-all-done.2, bf16[8,2,48,768]{3,2,0,1:T(8,128)(2,1)S(1)} %get-tuple-element.8, bf16[1,2,768,2048]{3,2,1,0:T(8,128)(2,1)S(1)} %bitcast.257), kind=kOutput, calls=%fused_computation.6 | convolution fusion | flops 2423782656 | bytes 10618368 | tf_op jit(solution)/shard_map/sjcf,jfd->sjcd/dot_general | solution.py:77
  251.1 18.4 %all-to-all-start.5 = ((bf16[8,2,48]{2,1,0:T(2,128)(2,1)}), bf16[8,2,48]{2,1,0:T(2,128)(2,1)S(1)}, u32[]{:S(2)}, u32[]{:S(2)}) async-start(bf16[8,2,48]{2,1,0:T(2,128)(2,1)} %copy.212), calls=%async_computation.5 | async-start | bytes 8192 | tf_op jit(solution)/shard_map/all_to_all | solution.py:170
  269.5 11.3 %fusion.31 = bf16[8,2,48,2048]{3,2,0,1:T(8,128)(2,1)S(1)} fusion(bf16[1,2,768,2048]{3,2,1,0:T(8,128)(2,1)} %param.17, f32[2,8,48,768]{3,2,1,0:T(8,128)} %fusion.9, bf16[8,2,48,2048]{3,2,0,1:T(8,128)(2,1)} %copy-done.3, bf16[1,2,2048,768]{3,2,1,0:T(8,128)(2,1)} %param.16), kind=kOutput, calls=%fused_computation.34 | convolution fusion | flops 4836950016 | bytes 21233664 | tf_op jit(solution)/shard_map/sjcf,jfd->sjcd/dot_general | solution.py:77
  280.8 2.1 copy.201
  282.9 6.0 %all-to-all-start = ((bf16[8,2,48,2048]{3,2,1,0:T(8,128)(2,1)}), bf16[8,2,48,2048]{3,2,1,0:T(8,128)(2,1)S(1)}, u32[]{:S(2)}, u32[]{:S(2)}) async-start(bf16[8,2,48,2048]{3,2,1,0:T(8,128)(2,1)} %copy.201), calls=%async_computation | async-start | bytes 6291456 | tf_op jit(solution)/shard_map/all_to_all | solution.py:115
  288.9 5.2 %fusion.5 = f32[2,8,48,2048]{3,2,1,0:T(8,128)S(1)} fusion(bf16[8,2,48,768]{3,2,0,1:T(8,128)(2,1)} %get-tuple-element.9, bf16[1,2,2048,768]{3,2,1,0:T(8,128)(2,1)} %param.15), kind=kOutput, calls=%fused_computation.10 | convolution fusion | flops 2415919104 | bytes 13762560 | tf_op jit(solution)/shard_map/sjcf,jdf->sjcd/dot_general | solution.py:153
  294.1 7.3 %fusion.34 = bf16[8,2,48,2048]{3,2,0,1:T(8,128)(2,1)S(1)} fusion(f32[2,8,48,2048]{3,2,1,0:T(8,128)S(1)} %fusion.5, bf16[8,2,48,768]{3,2,0,1:T(8,128)(2,1)S(1)} %copy-done.10, bf16[1,2,2048,768]{3,2,1,0:T(8,128)(2,1)} %param.16), kind=kOutput, calls=%fused_computation.35 | convolution fusion | flops 2419064832 | bytes 16908288 | tf_op jit(solution)/shard_map/sjcf,jdf->sjcd/dot_general | solution.py:154
  301.4 1.9 copy.211
  303.3 55.9 %all-to-all-done = bf16[8,2,48,2048]{3,2,1,0:T(8,128)(2,1)S(1)} async-done(((bf16[8,2,48,2048]{3,2,1,0:T(8,128)(2,1)}), bf16[8,2,48,2048]{3,2,1,0:T(8,128)(2,1)S(1)}, u32[]{:S(2)}, u32[]{:S(2)}) %all-to-all-start) | async-done | bytes 3145760 | tf_op jit(solution)/shard_map/all_to_all | solution.py:115
  359.2 4.7 %all-to-all-start.4 = ((bf16[8,2,48,2048]{3,2,1,0:T(8,128)(2,1)}), bf16[8,2,48,2048]{3,2,1,0:T(8,128)(2,1)}, u32[]{:S(2)}, u32[]{:S(2)}) async-start(bf16[8,2,48,2048]{3,2,1,0:T(8,128)(2,1)} %copy.211), calls=%async_computation.4 | async-start | bytes 6291456 | tf_op jit(solution)/shard_map/all_to_all | solution.py:169
  364.0 8.6 %fusion.4 = bf16[1,2,768,2048]{3,2,1,0:T(8,128)(2,1)} fusion(bf16[8,2,48,768]{3,2,0,1:T(8,128)(2,1)} %copy-done.14, f32[8,2,48]{2,0,1:T(8,128)S(1)} %copy_convert_fusion, bf16[8,2,48,2048]{3,2,1,0:T(8,128)(2,1)} %all-to-all-done.2), kind=kOutput, calls=%fused_computation.9 | convolution fusion | flops 2423783424 | bytes 10619904 | tf_op jit(solution)/shard_map/sjcf,sjcd->jfd/dot_general | solution.py:162
  372.6 5.4 %fusion.2 = bf16[1,2,2048,768]{3,2,1,0:T(8,128)(2,1)} fusion(bf16[8,2,48,2048]{3,2,1,0:T(8,128)(2,1)S(1)} %copy-done.2, bf16[8,2,48,768]{3,2,0,1:T(8,128)(2,1)S(1)} %copy-done.12), kind=kOutput, calls=%fused_computation.7 | convolution fusion | flops 2419064832 | bytes 10616832 | tf_op jit(solution)/shard_map/sjcd,sjcf->jdf/dot_general | solution.py:156
  378.0 5.4 %fusion.3 = bf16[1,2,2048,768]{3,2,1,0:T(8,128)(2,1)} fusion(bf16[8,2,48,2048]{3,2,1,0:T(8,128)(2,1)S(1)} %copy-done.2, bf16[8,2,48,768]{3,2,0,1:T(8,128)(2,1)S(1)} %copy-done.11), kind=kOutput, calls=%fused_computation.8 | convolution fusion | flops 2419064832 | bytes 10616832 | tf_op jit(solution)/shard_map/sjcd,sjcf->jdf/dot_general | solution.py:159
  384.1 3.2 fusion.64
  388.7 2.4 fusion.55
  391.1 42.9 %all-to-all-done.4 = bf16[8,2,48,2048]{3,2,1,0:T(8,128)(2,1)} async-done(((bf16[8,2,48,2048]{3,2,1,0:T(8,128)(2,1)}), bf16[8,2,48,2048]{3,2,1,0:T(8,128)(2,1)}, u32[]{:S(2)}, u32[]{:S(2)}) %all-to-all-start.4) | async-done | bytes 3145760 | tf_op jit(solution)/shard_map/all_to_all | solution.py:169
  434.0 2.7 fusion.76
  436.7 1.9 fusion.86
  (94 shorter events, 14.1 us)
Async XLA Ops:
  5.1 13.7 %all-to-all-start.1 = ((bf16[8,2,48]{2,1,0:T(2,128)(2,1)}), bf16[8,2,48]{2,1,0:T(2,128)(2,1)S(1)}, u32[]{:S(2)}, u32[]{:S(2)}) async-start(bf16[8,2,48]{2,1,0:T(2,128)(2,1)} %reshape.169), calls=%async_computation.1 | async-start | bytes 8192 | tf_op jit(solution)/shard_map/all_to_all | solution.py:137
  12.5 6.3 %copy-start.5 = (s32[64,8]{1,0:T(8,128)}, s32[64,8]{1,0:T(8,128)S(1)}, u32[]{:S(2)}) copy-start(s32[64,8]{1,0:T(8,128)S(1)} %bitcast_add_fusion) | copy-start | bytes 6148
  14.9 3.9 copy-start.7
  18.9 6.3 %copy-start.9 = (s32[1,64,8]{1,2,0:T(8,128)S(1)}, s32[1,64,8]{1,2,0:T(8,128)}, u32[]{:S(2)}) copy-start(s32[1,64,8]{1,2,0:T(8,128)} %param.18) | copy-start | bytes 6148
  18.9 75.9 %all-to-all-start.3 = ((bf16[8,2,48,2048]{3,2,1,0:T(8,128)(2,1)}), bf16[8,2,48,2048]{3,2,1,0:T(8,128)(2,1)S(1)}, u32[]{:S(2)}, u32[]{:S(2)}) async-start(bf16[8,2,48,2048]{3,2,1,0:T(8,128)(2,1)} %bitcast.29), calls=%async_computation.3 | async-start | bytes 6291456 | tf_op jit(solution)/shard_map/all_to_all | solution.py:135
  24.6 6.2 %collective-permute-start.8 = (bf16[1,64,2048]{2,1,0:T(8,128)(2,1)}, bf16[1,64,2048]{2,1,0:T(8,128)(2,1)}, u32[]{:S(2)}, u32[]{:S(2)}) collective-permute-start(bf16[1,64,2048]{2,1,0:T(8,128)(2,1)} %param.13), channel_id=1, source_target_pairs={{0,24},{8,0},{16,8},{24,16},{1,25},{9,1},{17,9},{25,17},{2,26},{10... | collective-permute-start | bytes 786440 | tf_op jit(solution)/shard_map/ppermute | solution.py:28
  24.7 83.1 %collective-permute-start = (bf16[1,64,2048]{2,1,0:T(8,128)(2,1)}, bf16[1,64,2048]{2,1,0:T(8,128)(2,1)S(1)}, u32[]{:S(2)}, u32[]{:S(2)}) collective-permute-start(bf16[1,64,2048]{2,1,0:T(8,128)(2,1)} %param.11), channel_id=1, source_target_pairs={{0,8},{8,16},{16,24},{24,0},{1,9},{9,17},{17,25},{25,1},{2,10},{10... | collective-permute-start | bytes 786440 | tf_op jit(solution)/shard_map/ppermute | solution.py:28
  94.8 143.4 %copy-start.1 = (bf16[8,2,48,2048]{3,2,1,0:T(8,128)(2,1)}, bf16[8,2,48,2048]{3,2,1,0:T(8,128)(2,1)S(1)}, u32[]{:S(2)}) copy-start(bf16[8,2,48,2048]{3,2,1,0:T(8,128)(2,1)S(1)} %all-to-all-done.3) | copy-start | bytes 9437188
  94.8 136.9 %all-to-all-start.2 = ((bf16[8,2,48,2048]{3,2,1,0:T(8,128)(2,1)}), bf16[8,2,48,2048]{3,2,1,0:T(8,128)(2,1)}, u32[]{:S(2)}, u32[]{:S(2)}) async-start(bf16[8,2,48,2048]{3,2,1,0:T(8,128)(2,1)} %bitcast.25), calls=%async_computation.2 | async-start | bytes 6291456 | tf_op jit(solution)/shard_map/all_to_all | solution.py:136
  107.8 1.5 copy-start.4
  109.0 114.6 %slice-start.2 = ((s8[6291456]{0:T(1024)(128)(4,1)}), s8[4194304]{0:T(1024)(128)(4,1)S(1)}, s32[]{:S(2)}) async-start(s8[6291456]{0:T(1024)(128)(4,1)} %bitcast.258), calls=%async_computation.8 | async-start | bytes 8388608
  109.3 24.6 %collective-permute-start.1 = (bf16[1,2,48,2048]{3,2,0,1:T(8,128)(2,1)S(1)}, bf16[1,2,48,2048]{3,2,0,1:T(8,128)(2,1)S(1)}, u32[]{:S(2)}, u32[]{:S(2)}) collective-permute-start(bf16[1,2,48,2048]{3,2,0,1:T(8,128)(2,1)S(1)} %get-tuple-element.17), channel_id=1, source_target_pairs={{0,1},{1,0},{2,3},{3,2},{4,5},{5,4},{6,7},{7,6},{8,9},{9,8},{10,11... | collective-permute-start | bytes 1179656 | tf_op jit(solution)/shard_map/ppermute | solution.py:21
  111.1 49.3 %collective-permute-start.2 = (bf16[1,2,48,2048]{3,2,0,1:T(8,128)(2,1)S(1)}, bf16[1,2,48,2048]{3,2,0,1:T(8,128)(2,1)S(1)}, u32[]{:S(2)}, u32[]{:S(2)}) collective-permute-start(bf16[1,2,48,2048]{3,2,0,1:T(8,128)(2,1)S(1)} %get-tuple-element.16), channel_id=1, source_target_pairs={{0,2},{1,3},{2,0},{3,1},{4,6},{5,7},{6,4},{7,5},{8,10},{9,11},{10,... | collective-permute-start | bytes 1179656 | tf_op jit(solution)/shard_map/ppermute | solution.py:21
  112.6 56.3 %collective-permute-start.3 = (bf16[1,2,48,2048]{3,2,0,1:T(8,128)(2,1)S(1)}, bf16[1,2,48,2048]{3,2,0,1:T(8,128)(2,1)S(1)}, u32[]{:S(2)}, u32[]{:S(2)}) collective-permute-start(bf16[1,2,48,2048]{3,2,0,1:T(8,128)(2,1)S(1)} %get-tuple-element.15), channel_id=1, source_target_pairs={{0,3},{1,2},{2,1},{3,0},{4,7},{5,6},{6,5},{7,4},{8,11},{9,10},{10,... | collective-permute-start | bytes 1179656 | tf_op jit(solution)/shard_map/ppermute | solution.py:21
  112.9 100.5 %collective-permute-start.4 = (bf16[1,2,48,2048]{3,2,0,1:T(8,128)(2,1)S(1)}, bf16[1,2,48,2048]{3,2,0,1:T(8,128)(2,1)S(1)}, u32[]{:S(2)}, u32[]{:S(2)}) collective-permute-start(bf16[1,2,48,2048]{3,2,0,1:T(8,128)(2,1)S(1)} %get-tuple-element.14), channel_id=1, source_target_pairs={{0,4},{1,5},{2,6},{3,7},{4,0},{5,1},{6,2},{7,3},{8,12},{9,13},{10,... | collective-permute-start | bytes 1179656 | tf_op jit(solution)/shard_map/ppermute | solution.py:21
  115.5 108.1 %slice-start.3 = ((s8[6291456]{0:T(1024)(128)(4,1)}), s8[2097152]{0:T(1024)(128)(4,1)S(1)}, s32[]{:S(2)}) async-start(s8[6291456]{0:T(1024)(128)(4,1)} %bitcast.258), calls=%async_computation.9 | async-start | bytes 4194304
  115.5 106.3 %collective-permute-start.5 = (bf16[1,2,48,2048]{3,2,0,1:T(8,128)(2,1)S(1)}, bf16[1,2,48,2048]{3,2,0,1:T(8,128)(2,1)S(1)}, u32[]{:S(2)}, u32[]{:S(2)}) collective-permute-start(bf16[1,2,48,2048]{3,2,0,1:T(8,128)(2,1)S(1)} %get-tuple-element.13), channel_id=1, source_target_pairs={{0,5},{1,4},{2,7},{3,6},{4,1},{5,0},{6,3},{7,2},{8,13},{9,12},{10,... | collective-permute-start | bytes 1179656 | tf_op jit(solution)/shard_map/ppermute | solution.py:21
  133.9 87.9 %collective-permute-start.6 = (bf16[1,2,48,2048]{3,2,0,1:T(8,128)(2,1)S(1)}, bf16[1,2,48,2048]{3,2,0,1:T(8,128)(2,1)S(1)}, u32[]{:S(2)}, u32[]{:S(2)}) collective-permute-start(bf16[1,2,48,2048]{3,2,0,1:T(8,128)(2,1)S(1)} %get-tuple-element.12), channel_id=1, source_target_pairs={{0,6},{1,7},{2,4},{3,5},{4,2},{5,3},{6,0},{7,1},{8,14},{9,15},{10,... | collective-permute-start | bytes 1179656 | tf_op jit(solution)/shard_map/ppermute | solution.py:21
  160.4 61.5 %collective-permute-start.7 = (bf16[1,2,48,2048]{3,2,0,1:T(8,128)(2,1)S(1)}, bf16[1,2,48,2048]{3,2,0,1:T(8,128)(2,1)S(1)}, u32[]{:S(2)}, u32[]{:S(2)}) collective-permute-start(bf16[1,2,48,2048]{3,2,0,1:T(8,128)(2,1)S(1)} %get-tuple-element.11), channel_id=1, source_target_pairs={{0,7},{1,6},{2,5},{3,4},{4,3},{5,2},{6,1},{7,0},{8,15},{9,14},{10,... | collective-permute-start | bytes 1179656 | tf_op jit(solution)/shard_map/ppermute | solution.py:21
  221.9 1.7 copy-start.3
  231.7 6.5 %copy-start.13 = (f32[2,8,48,768]{3,2,1,0:T(8,128)S(1)}, f32[2,8,48,768]{3,2,1,0:T(8,128)}, u32[]{:S(2)}) copy-start(f32[2,8,48,768]{3,2,1,0:T(8,128)} %fusion.7) | copy-start | bytes 7077892
  231.7 14.0 %slice-start = ((s8[6291456]{0:T(1024)(128)(4,1)}), s8[2097152]{0:T(1024)(128)(4,1)S(1)}, s32[]{:S(2)}) async-start(s8[6291456]{0:T(1024)(128)(4,1)} %bitcast.256), calls=%async_computation.6 | async-start | bytes 4194304
  238.2 7.4 %slice-start.1 = ((s8[6291456]{0:T(1024)(128)(4,1)}), s8[4194304]{0:T(1024)(128)(4,1)S(1)}, s32[]{:S(2)}) async-start(s8[6291456]{0:T(1024)(128)(4,1)} %bitcast.256), calls=%async_computation.7 | async-start | bytes 8388608
  245.7 4.8 %copy-start.14 = (bf16[8,2,48,768]{3,2,0,1:T(8,128)(2,1)}, bf16[8,2,48,768]{3,2,0,1:T(8,128)(2,1)S(1)}, u32[]{:S(2)}) copy-start(bf16[8,2,48,768]{3,2,0,1:T(8,128)(2,1)S(1)} %get-tuple-element.8) | copy-start | bytes 3538948
  251.1 31.8 %all-to-all-start.5 = ((bf16[8,2,48]{2,1,0:T(2,128)(2,1)}), bf16[8,2,48]{2,1,0:T(2,128)(2,1)S(1)}, u32[]{:S(2)}, u32[]{:S(2)}) async-start(bf16[8,2,48]{2,1,0:T(2,128)(2,1)} %copy.212), calls=%async_computation.5 | async-start | bytes 8192 | tf_op jit(solution)/shard_map/all_to_all | solution.py:170
  282.9 76.3 %all-to-all-start = ((bf16[8,2,48,2048]{3,2,1,0:T(8,128)(2,1)}), bf16[8,2,48,2048]{3,2,1,0:T(8,128)(2,1)S(1)}, u32[]{:S(2)}, u32[]{:S(2)}) async-start(bf16[8,2,48,2048]{3,2,1,0:T(8,128)(2,1)} %copy.201), calls=%async_computation | async-start | bytes 6291456 | tf_op jit(solution)/shard_map/all_to_all | solution.py:115
  288.9 5.2 %copy-start.10 = (bf16[8,2,48,768]{3,2,0,1:T(8,128)(2,1)S(1)}, bf16[8,2,48,768]{3,2,0,1:T(8,128)(2,1)}, u32[]{:S(2)}) copy-start(bf16[8,2,48,768]{3,2,0,1:T(8,128)(2,1)} %get-tuple-element.10) | copy-start | bytes 3538948
  359.2 74.8 %all-to-all-start.4 = ((bf16[8,2,48,2048]{3,2,1,0:T(8,128)(2,1)}), bf16[8,2,48,2048]{3,2,1,0:T(8,128)(2,1)}, u32[]{:S(2)}, u32[]{:S(2)}) async-start(bf16[8,2,48,2048]{3,2,1,0:T(8,128)(2,1)} %copy.211), calls=%async_computation.4 | async-start | bytes 6291456 | tf_op jit(solution)/shard_map/all_to_all | solution.py:169
  363.9 8.7 %copy-start.2 = (bf16[8,2,48,2048]{3,2,1,0:T(8,128)(2,1)S(1)}, bf16[8,2,48,2048]{3,2,1,0:T(8,128)(2,1)}, u32[]{:S(2)}) copy-start(bf16[8,2,48,2048]{3,2,1,0:T(8,128)(2,1)} %copy-done.1) | copy-start | bytes 9437188
  363.9 8.7 %copy-start.12 = (bf16[8,2,48,768]{3,2,0,1:T(8,128)(2,1)S(1)}, bf16[8,2,48,768]{3,2,0,1:T(8,128)(2,1)}, u32[]{:S(2)}) copy-start(bf16[8,2,48,768]{3,2,0,1:T(8,128)(2,1)} %get-tuple-element.9) | copy-start | bytes 3538948
  372.6 5.4 %copy-start.11 = (bf16[8,2,48,768]{3,2,0,1:T(8,128)(2,1)S(1)}, bf16[8,2,48,768]{3,2,0,1:T(8,128)(2,1)}, u32[]{:S(2)}) copy-start(bf16[8,2,48,768]{3,2,0,1:T(8,128)(2,1)} %get-tuple-element.10) | copy-start | bytes 3538948
  378.0 6.1 %copy-start.6 = (s32[64,8]{1,0:T(8,128)S(1)}, s32[64,8]{1,0:T(8,128)}, u32[]{:S(2)}) copy-start(s32[64,8]{1,0:T(8,128)} %copy-done.5) | copy-start | bytes 6148
  383.4 50.6 %copy-start = (bf16[1,64,2048]{2,1,0:T(8,128)(2,1)S(1)}, bf16[1,64,2048]{2,1,0:T(8,128)(2,1)}, u32[]{:S(2)}) copy-start(bf16[1,64,2048]{2,1,0:T(8,128)(2,1)} %param.12) | copy-start | bytes 786436
  383.4 50.6 %copy-start.8 = (f32[64]{0:T(128)S(1)}, f32[64]{0:T(128)}, u32[]{:S(2)}) copy-start(f32[64]{0:T(128)} %copy-done.7) | copy-start | bytes 772
